TPU v7x, 128 devices: a whole 4x4x4 slice. The times are simulated.
128 devices in a mesh: gx: 8 (over y, core), gy: 16 (over x, z).
Axes of the slice: x: 4, y: 4, z: 4, core: 2. Of those that a mesh axis runs over, the one named last changes fastest.
Arguments:
- voxels: bfloat16 [1024, 512, 128], P(('gx', 'gy')), may hold values from -6 to 6
- neighbours: int32 [1024, 6], P(('gx', 'gy')), may hold values from -1 to 7, as said below
- block_count: int32 [128], P(('gx', 'gy')), may hold values from 1 to 8, as said below
- conv_weight: bfloat16 [27, 128, 128], replicated, may hold values from -0.109375 to 0.109375
- qkv_weight: bfloat16 [128, 384], replicated, may hold values from -10 to 10
- out_weight: bfloat16 [128, 128], replicated, may hold values from -0.5 to 0.5
Outputs:
- refined: bfloat16 [1024, 512, 128], P(('gx', 'gy'))
Inputs may be any that keep to these rules, and one draw needn't show every extreme that they name: `neighbours`: each device holds one scene column of blocks at distinct heights of 16, in slots 0 to block_count - 1 in rising height. Entries name the face neighbour's slot on its own device (the x faces on the device one index lower or higher along gx, the y faces along gy, the z faces on the same device), or -1 where that neighbour is not active; the relation is mutual, and rows of unused slots are -1. `block_count`: some device holds 8 active blocks.
All inputs are finite; a program needn't handle non-finite values.
Results may differ from a plain program's by a relative error of at most 0.013.
Values may be sent and summed in bfloat16 or wider, within the bound.
A program may use at most 128 MiB of HBM per device.

v0:
```python
import math

import jax
import jax.numpy as jnp
from jax import lax
from jax.sharding import PartitionSpec as P

HEADS = 4
SIDE = 8


def passed_along(value, axis, steps):
    count = lax.axis_size(axis)
    initial, last = (max(0, -steps), min(count, count - steps))
    return lax.ppermute(value, axis, [(source, source + steps) for source in range(initial, last)])


def with_halo(x, sides, width):
    edges = {}
    for axis, dim in sides:
        peers, length = (lax.axis_size(axis), x.shape[dim])
        up = [(i, (i + 1) % peers) for i in range(peers - 1)]
        last = lax.slice_in_dim(x, length - width, length, axis=dim)
        initial = lax.slice_in_dim(x, 0, width, axis=dim)
        edges[dim] = (
            lax.ppermute(last, axis, up),
            lax.ppermute(initial, axis, [(b, a) for a, b in up]),
        )
    done = []
    for _, dim in sides:
        low, high = edges[dim]
        around = [(width, width) if d in done else (0, 0) for d in range(x.ndim)]
        x = jnp.concatenate([jnp.pad(low, around), x, jnp.pad(high, around)], axis=dim)
        done.append(dim)
    return x


def pick_rows(lookup, slot_index):
    slots = lookup.shape[0]
    onehot = (slot_index[:, None] == jnp.arange(slots, dtype=jnp.int32)[None, :]).astype(
        lookup.dtype
    )
    flattened = lookup.reshape(slots, -1)
    chosen = jnp.dot(onehot, flattened, preferred_element_type=jnp.float32).astype(lookup.dtype)
    return chosen.reshape((slot_index.shape[0],) + lookup.shape[1:])


def padded_cells(block_cubes, face_cells):
    padded = jnp.pad(block_cubes, ((0, 0), (1, 1), (1, 1), (1, 1), (0, 0)))
    padded = padded.at[:, 0, 1:-1, 1:-1].set(face_cells[0])
    padded = padded.at[:, -1, 1:-1, 1:-1].set(face_cells[1])
    padded = padded.at[:, 1:-1, 0, 1:-1].set(face_cells[2])
    padded = padded.at[:, 1:-1, -1, 1:-1].set(face_cells[3])
    padded = padded.at[:, 1:-1, 1:-1, 0].set(face_cells[4])
    padded = padded.at[:, 1:-1, 1:-1, -1].set(face_cells[5])
    return padded


def convolve(padded, conv_weight):
    channels = padded.shape[-1]
    running = jnp.zeros((padded.shape[0] * SIDE**3, conv_weight.shape[2]), jnp.float32)
    tap_index = 0
    for step_x in range(3):
        for step_y in range(3):
            for step_z in range(3):
                window = padded[
                    :, step_x : step_x + SIDE, step_y : step_y + SIDE, step_z : step_z + SIDE
                ].reshape(-1, channels)
                running = running + jnp.dot(
                    window, conv_weight[tap_index], preferred_element_type=jnp.float32
                )
                tap_index = tap_index + 1
    return running


def project(row_data, weight):
    values = row_data.astype(jnp.float32)
    mean_square = jnp.mean(values * values, axis=-1, keepdims=True)
    guarded = mean_square + 1e-06
    inverse = lax.rsqrt(guarded)
    normed = (values * inverse).astype(jnp.bfloat16)
    return jnp.dot(normed, weight, preferred_element_type=jnp.float32).astype(jnp.bfloat16)


def attend_block(queries, key_rows, value_rows, key_ok):
    voxel_count, channels = queries.shape
    head_width = channels // HEADS
    q_heads = queries.reshape(voxel_count, HEADS, head_width)
    k_heads = key_rows.reshape(-1, HEADS, head_width)
    v_heads = value_rows.reshape(-1, HEADS, head_width)
    scores = jnp.einsum(
        "qhd,khd->hqk", q_heads, k_heads, preferred_element_type=jnp.float32
    ) / math.sqrt(head_width)
    key_mask = jnp.repeat(key_ok, voxel_count)
    scores = jnp.where(key_mask[None, None, :], scores, jnp.float32(-1e30))
    row_max = jnp.max(scores, axis=-1, keepdims=True)
    weights = jnp.exp(scores - row_max)
    probabilities = (weights / jnp.sum(weights, axis=-1, keepdims=True)).astype(jnp.bfloat16)
    mixture = jnp.einsum("hqk,khd->qhd", probabilities, v_heads, preferred_element_type=jnp.float32)
    return mixture.reshape(voxel_count, channels).astype(jnp.bfloat16)


def select_sets(pool, grid_ids, neighbours):
    tiles, blocks = (pool.shape[0], pool.shape[1])
    own_slots = jnp.arange(blocks, dtype=jnp.int32)[:, None]
    slot_table = jnp.concatenate([own_slots, neighbours], axis=1)
    wanted = jnp.where(slot_table >= 0, grid_ids[None, :] * blocks + slot_table, -1)
    onehot = (
        wanted.reshape(-1)[:, None] == jnp.arange(tiles * blocks, dtype=jnp.int32)[None, :]
    ).astype(pool.dtype)
    flattened = pool.reshape(tiles * blocks, -1)
    chosen = jnp.dot(onehot, flattened, preferred_element_type=jnp.float32).astype(pool.dtype)
    return chosen.reshape((blocks, 7) + pool.shape[2:])


def body(voxels, neighbours, block_count, conv_weight, qkv_weight, out_weight):
    blocks, voxel_count, channels = voxels.shape
    block_cubes = voxels.reshape(blocks, SIDE, SIDE, SIDE, channels)
    received = []
    for offset, outgoing in ((1, block_cubes[:, -1]), (-1, block_cubes[:, 0])):
        received.append(passed_along(outgoing, "gx", offset))
    for offset, outgoing in ((1, block_cubes[:, :, -1]), (-1, block_cubes[:, :, 0])):
        received.append(passed_along(outgoing, "gy", offset))
    face_cells = [
        pick_rows(received[face_index], neighbours[:, face_index]) for face_index in range(4)
    ]
    face_cells.append(pick_rows(block_cubes[:, :, :, -1], neighbours[:, 4]))
    face_cells.append(pick_rows(block_cubes[:, :, :, 0], neighbours[:, 5]))
    padded = padded_cells(block_cubes, face_cells)
    conv_sum = convolve(padded, conv_weight)
    mixed_in = (voxels.reshape(-1, channels).astype(jnp.float32) + conv_sum).astype(jnp.bfloat16)
    packed = project(mixed_in, qkv_weight)
    queries = packed[:, :channels].reshape(blocks, voxel_count, channels)
    key_values = packed[:, channels:].reshape(blocks, voxel_count, 2 * channels)
    beside = with_halo(key_values[None, None], (("gx", 0), ("gy", 1)), 1)
    pool = beside.reshape(9, blocks, voxel_count, 2 * channels)
    grid_ids = jnp.array([4, 1, 7, 3, 5, 4, 4], dtype=jnp.int32)
    key_sets = select_sets(pool, grid_ids, neighbours)
    key_ok = jnp.concatenate([jnp.ones((blocks, 1), dtype=bool), neighbours >= 0], axis=1)

    def one_block(block_items):
        block_queries, block_pairs, block_ok = block_items
        return attend_block(
            block_queries, block_pairs[..., :channels], block_pairs[..., channels:], block_ok
        )

    attended = lax.map(one_block, (queries, key_sets, key_ok))
    result = mixed_in.astype(jnp.float32) + jnp.dot(
        attended.reshape(-1, channels), out_weight, preferred_element_type=jnp.float32
    )
    active = jnp.arange(blocks, dtype=jnp.int32) < block_count[0]
    result = jnp.where(
        active[:, None, None], result.reshape(blocks, voxel_count, channels), jnp.float32(0.0)
    )
    return result.astype(jnp.bfloat16)


def solution(mesh):
    placed = (P(("gx", "gy"), None, None), P(("gx", "gy"), None), P(("gx", "gy")), P(), P(), P())
    return jax.shard_map(
        body, mesh=mesh, in_specs=placed, out_specs=P(("gx", "gy"), None, None), check_vma=False
    )
```

profile of v0, /device:TPU:67, one launch (start us, length us, event | category | flops | bytes accessed | tf_op | source)
XLA Modules:
  0.0 499.6 jit_solution(10481251627513969367)
XLA Ops:
  1.8 3.8 collective-permute-start
  9.2 3.2 collective-permute-start.2
  14.5 3.8 slice_reduce_fusion
  33.1 6.2 %scatter.26 = bf16[8,10,10,10,128]{4,3,2,1,0:T(8,128)(2,1)S(1)} dynamic-update-slice(bf16[8,10,10,10,128]{4,3,2,1,0:T(8,128)(2,1)S(1)} %scatter.25, bf16[8,8,8,1,128]{4,3,2,1,0:T(2,128)(2,1)} %copy.21, s32[]{:T(128)} %copy.89, s32[]{:T(128)} %constant.236.clone.1, s32[]{:T(128)} %constant.236.clone.1, s32[]{:T(128)} %copy.89, s32[]{:T(128)} %copy.89) | dynamic-update-slice | bytes 262148 | tf_op jit(solution)/shard_map/scatter | solution.py:54
  39.4 6.2 %scatter.29 = bf16[8,10,10,10,128]{4,3,2,1,0:T(8,128)(2,1)S(1)} dynamic-update-slice(bf16[8,10,10,10,128]{4,3,2,1,0:T(8,128)(2,1)S(1)} %scatter.26, bf16[8,8,8,1,128]{4,3,2,1,0:T(2,128)(2,1)} %copy.23, s32[]{:T(128)} %copy.89, s32[]{:T(128)} %constant.236.clone.1, s32[]{:T(128)} %constant.236.clone.1, s32[]{:T(128)} %constant.237.clone.1, s32[]{:T(128)} %copy.89) | dynamic-update-slice | bytes 262148 | tf_op jit(solution)/shard_map/scatter | solution.py:55
  45.6 3.8 fusion.96
  49.4 8.1 %fusion.95 = (bf16[8,8,8,8,128]{4,3,2,1,0:T(8,128)(2,1)}, bf16[8,8,8,8,128]{4,3,2,1,0:T(8,128)(2,1)}, bf16[8,8,8,8,128]{4,3,2,1,0:T(8,128)(2,1)}, bf16[8,8,8,8,1...) fusion(bf16[8,10,10,10,128]{4,3,2,1,0:T(8,128)(2,1)S(1)} %scatt, ...), kind=kLoop, calls=%fused_computation.165 | loop fusion | bytes 39845888 | tf_op jit(solution)/shard_map/slice | solution.py:66
  95.9 3.4 collective-permute-start.4
  101.2 4.8 collective-permute-start.5
  108.5 35.0 %collective-permute-done.7 = bf16[1,1,8,512,256]{4,3,2,1,0:T(8,128)(2,1)} collective-permute-done((bf16[1,1,8,512,256]{4,3,2,1,0:T(8,128)(2,1)}, bf16[1,1,8,512,256]{4,3,2,1,0:T(8,128)(2,1)}, u32[]{:S(2)}, u32[]{:S(2)}) %collective-permute-start.7) | collective-permute-done | bytes 2097184 | tf_op jit(solution)/shard_map/ppermute | solution.py:27
  145.4 6.3 %fusion.13 = bf16[3,3,8,512,256]{4,3,2,1,0:T(8,128)(2,1)S(1)} fusion(bf16[1,1,8,512,256]{4,3,2,1,0:T(8,128)(2,1)} %collective-permute-done.7, bf16[1,1,8,512,256]{4,3,2,1,0:T(8,128)(2,1)} %collective-permute-done.4, bf16[1,1,8,512,256]{4,3,2,1,0:T(8,128)(2,1)} %collective-permute-done.6, bf16[1,1,8,512,256]{4,3,2,1,0:T(8,128)(2,1)} %bitcast.72, ...), kind=kLoop, calls=%fused_computation.22 | loop fusion | flops 132120576 | bytes 29360128 | tf_op jit(solution)/shard_map/concatenate | solution.py:33
  151.7 12.0 %copy.42 = bf16[9,8,512,256]{3,1,2,0:T(8,128)(2,1)} copy(bf16[9,8,512,256]{3,2,1,0:T(8,128)(2,1)S(1)} %bitcast.232) | data formatting | bytes 37748736
  163.7 11.4 %convolution_convert_fusion = bf16[56,131072]{1,0:T(8,128)(2,1)} fusion(bf16[72,131072]{1,0:T(8,128)(2,1)} %bitcast.231, s32[56]{0:T(128)S(1)} %select_n.20), kind=kOutput, calls=%fused_computation.17 | convolution fusion | flops 1064308672 | bytes 33554656 | tf_op jit(solution)/shard_map/dot_general | solution.py:112
  175.1 14.7 %copy.43 = bf16[7,8,512,256]{3,2,1,0:T(8,128)(2,1)} copy(bf16[7,8,512,256]{3,1,2,0:T(8,128)(2,1)} %bitcast.233) | data formatting | bytes 29360128
  189.8 306.2 %while.16 = (s32[]{:T(128)}, bf16[8,512,128]{2,1,0:T(8,128)(2,1)}, bf16[8,7,512,256]{3,2,1,0:T(8,128)(2,1)}, pred[8,7]{1,0:T(8,128)(4,1)S(1)}, bf16[8,512,128]{2,1,0:T(8,128)(2,1)}, /*index=5*/s32[]{:T(128)}) while((s32[]{:T(128)}, bf16[8,512,128]{2,1,0:T(8,128)(2,1)}, bf16[8,7,512,256]{3,2,1,0:T(8,128)(2,1)}, pred[8,7]{1,0:T(8,128)(4,1)S(1)}, ...), condition=%wide.region_4.5_spmd, body=%wide.region_1.4_spmd.sunk | while | flops 983633408 | bytes 76576872 | solution.py:147
  189.8 2.9 constant_dynamic-slice_fusion.4
  192.7 3.3 copy.71
  201.6 14.0 %fusion.143 = (f32[4,512]{1,0:T(4,128)S(1)}, f32[4,512,3584]{2,1,0:T(8,128)}) fusion(pred[3584]{0:T(1024)(128)(4,1)S(1)} %broadcast_in_dim.79, bf16[512,4,32]{0,2,1:T(8,128)(2,1)S(1)} %bitcast.268, bf16[3584,4,32]{0,2,1:T(8,128)(2,1)S(1)} %reshape.506), kind=kOutput, calls=%fused_computation.164.clone.1 | convolution fusion | flops 499125760 | bytes 30420480 | tf_op jit(solution)/shard_map/while/body/eval_jaxpr/sub | solution.py:97
  215.5 11.8 %fusion.144 = bf16[4,32,512]{2,1,0:T(8,128)(2,1)S(1)} fusion(bf16[3584,4,32]{0,2,1:T(8,128)(2,1)S(1)} %reshape.505, f32[4,512,3584]{2,1,0:T(8,128)} %get-tuple-element.207, f32[4,512]{1,0:T(4,128)S(1)} %get-tuple-element.208), kind=kOutput, calls=%fused_computation.10.clone.1 | convolution fusion | flops 484507648 | bytes 30416896 | tf_op jit(solution)/shard_map/while/body/eval_jaxpr/hqk,khd->qhd/dot_general | solution.py:99
  228.1 2.9 constant_dynamic-slice_fusion.4
  230.9 3.3 copy.71
  239.9 13.9 %fusion.143 = (f32[4,512]{1,0:T(4,128)S(1)}, f32[4,512,3584]{2,1,0:T(8,128)}) fusion(pred[3584]{0:T(1024)(128)(4,1)S(1)} %broadcast_in_dim.79, bf16[512,4,32]{0,2,1:T(8,128)(2,1)S(1)} %bitcast.268, bf16[3584,4,32]{0,2,1:T(8,128)(2,1)S(1)} %reshape.506), kind=kOutput, calls=%fused_computation.164.clone.1 | convolution fusion | flops 499125760 | bytes 30420480 | tf_op jit(solution)/shard_map/while/body/eval_jaxpr/sub | solution.py:97
  253.8 11.8 %fusion.144 = bf16[4,32,512]{2,1,0:T(8,128)(2,1)S(1)} fusion(bf16[3584,4,32]{0,2,1:T(8,128)(2,1)S(1)} %reshape.505, f32[4,512,3584]{2,1,0:T(8,128)} %get-tuple-element.207, f32[4,512]{1,0:T(4,128)S(1)} %get-tuple-element.208), kind=kOutput, calls=%fused_computation.10.clone.1 | convolution fusion | flops 484507648 | bytes 30416896 | tf_op jit(solution)/shard_map/while/body/eval_jaxpr/hqk,khd->qhd/dot_general | solution.py:99
  266.4 2.9 constant_dynamic-slice_fusion.4
  269.2 3.3 copy.71
  278.1 13.9 %fusion.143 = (f32[4,512]{1,0:T(4,128)S(1)}, f32[4,512,3584]{2,1,0:T(8,128)}) fusion(pred[3584]{0:T(1024)(128)(4,1)S(1)} %broadcast_in_dim.79, bf16[512,4,32]{0,2,1:T(8,128)(2,1)S(1)} %bitcast.268, bf16[3584,4,32]{0,2,1:T(8,128)(2,1)S(1)} %reshape.506), kind=kOutput, calls=%fused_computation.164.clone.1 | convolution fusion | flops 499125760 | bytes 30420480 | tf_op jit(solution)/shard_map/while/body/eval_jaxpr/sub | solution.py:97
  292.1 11.8 %fusion.144 = bf16[4,32,512]{2,1,0:T(8,128)(2,1)S(1)} fusion(bf16[3584,4,32]{0,2,1:T(8,128)(2,1)S(1)} %reshape.505, f32[4,512,3584]{2,1,0:T(8,128)} %get-tuple-element.207, f32[4,512]{1,0:T(4,128)S(1)} %get-tuple-element.208), kind=kOutput, calls=%fused_computation.10.clone.1 | convolution fusion | flops 484507648 | bytes 30416896 | tf_op jit(solution)/shard_map/while/body/eval_jaxpr/hqk,khd->qhd/dot_general | solution.py:99
  304.6 2.9 constant_dynamic-slice_fusion.4
  307.5 3.3 copy.71
  316.4 13.9 %fusion.143 = (f32[4,512]{1,0:T(4,128)S(1)}, f32[4,512,3584]{2,1,0:T(8,128)}) fusion(pred[3584]{0:T(1024)(128)(4,1)S(1)} %broadcast_in_dim.79, bf16[512,4,32]{0,2,1:T(8,128)(2,1)S(1)} %bitcast.268, bf16[3584,4,32]{0,2,1:T(8,128)(2,1)S(1)} %reshape.506), kind=kOutput, calls=%fused_computation.164.clone.1 | convolution fusion | flops 499125760 | bytes 30420480 | tf_op jit(solution)/shard_map/while/body/eval_jaxpr/sub | solution.py:97
  330.4 11.8 %fusion.144 = bf16[4,32,512]{2,1,0:T(8,128)(2,1)S(1)} fusion(bf16[3584,4,32]{0,2,1:T(8,128)(2,1)S(1)} %reshape.505, f32[4,512,3584]{2,1,0:T(8,128)} %get-tuple-element.207, f32[4,512]{1,0:T(4,128)S(1)} %get-tuple-element.208), kind=kOutput, calls=%fused_computation.10.clone.1 | convolution fusion | flops 484507648 | bytes 30416896 | tf_op jit(solution)/shard_map/while/body/eval_jaxpr/hqk,khd->qhd/dot_general | solution.py:99
  342.9 2.9 constant_dynamic-slice_fusion.4
  345.8 3.3 copy.71
  354.7 13.9 %fusion.143 = (f32[4,512]{1,0:T(4,128)S(1)}, f32[4,512,3584]{2,1,0:T(8,128)}) fusion(pred[3584]{0:T(1024)(128)(4,1)S(1)} %broadcast_in_dim.79, bf16[512,4,32]{0,2,1:T(8,128)(2,1)S(1)} %bitcast.268, bf16[3584,4,32]{0,2,1:T(8,128)(2,1)S(1)} %reshape.506), kind=kOutput, calls=%fused_computation.164.clone.1 | convolution fusion | flops 499125760 | bytes 30420480 | tf_op jit(solution)/shard_map/while/body/eval_jaxpr/sub | solution.py:97
  368.6 11.8 %fusion.144 = bf16[4,32,512]{2,1,0:T(8,128)(2,1)S(1)} fusion(bf16[3584,4,32]{0,2,1:T(8,128)(2,1)S(1)} %reshape.505, f32[4,512,3584]{2,1,0:T(8,128)} %get-tuple-element.207, f32[4,512]{1,0:T(4,128)S(1)} %get-tuple-element.208), kind=kOutput, calls=%fused_computation.10.clone.1 | convolution fusion | flops 484507648 | bytes 30416896 | tf_op jit(solution)/shard_map/while/body/eval_jaxpr/hqk,khd->qhd/dot_general | solution.py:99
  381.2 2.9 constant_dynamic-slice_fusion.4
  384.0 3.3 copy.71
  393.0 13.9 %fusion.143 = (f32[4,512]{1,0:T(4,128)S(1)}, f32[4,512,3584]{2,1,0:T(8,128)}) fusion(pred[3584]{0:T(1024)(128)(4,1)S(1)} %broadcast_in_dim.79, bf16[512,4,32]{0,2,1:T(8,128)(2,1)S(1)} %bitcast.268, bf16[3584,4,32]{0,2,1:T(8,128)(2,1)S(1)} %reshape.506), kind=kOutput, calls=%fused_computation.164.clone.1 | convolution fusion | flops 499125760 | bytes 30420480 | tf_op jit(solution)/shard_map/while/body/eval_jaxpr/sub | solution.py:97
  406.9 11.8 %fusion.144 = bf16[4,32,512]{2,1,0:T(8,128)(2,1)S(1)} fusion(bf16[3584,4,32]{0,2,1:T(8,128)(2,1)S(1)} %reshape.505, f32[4,512,3584]{2,1,0:T(8,128)} %get-tuple-element.207, f32[4,512]{1,0:T(4,128)S(1)} %get-tuple-element.208), kind=kOutput, calls=%fused_computation.10.clone.1 | convolution fusion | flops 484507648 | bytes 30416896 | tf_op jit(solution)/shard_map/while/body/eval_jaxpr/hqk,khd->qhd/dot_general | solution.py:99
  419.5 2.9 constant_dynamic-slice_fusion.4
  422.3 3.3 copy.71
  431.2 13.9 %fusion.143 = (f32[4,512]{1,0:T(4,128)S(1)}, f32[4,512,3584]{2,1,0:T(8,128)}) fusion(pred[3584]{0:T(1024)(128)(4,1)S(1)} %broadcast_in_dim.79, bf16[512,4,32]{0,2,1:T(8,128)(2,1)S(1)} %bitcast.268, bf16[3584,4,32]{0,2,1:T(8,128)(2,1)S(1)} %reshape.506), kind=kOutput, calls=%fused_computation.164.clone.1 | convolution fusion | flops 499125760 | bytes 30420480 | tf_op jit(solution)/shard_map/while/body/eval_jaxpr/sub | solution.py:97
  445.2 11.8 %fusion.144 = bf16[4,32,512]{2,1,0:T(8,128)(2,1)S(1)} fusion(bf16[3584,4,32]{0,2,1:T(8,128)(2,1)S(1)} %reshape.505, f32[4,512,3584]{2,1,0:T(8,128)} %get-tuple-element.207, f32[4,512]{1,0:T(4,128)S(1)} %get-tuple-element.208), kind=kOutput, calls=%fused_computation.10.clone.1 | convolution fusion | flops 484507648 | bytes 30416896 | tf_op jit(solution)/shard_map/while/body/eval_jaxpr/hqk,khd->qhd/dot_general | solution.py:99
  457.7 2.9 constant_dynamic-slice_fusion.4
  460.6 3.3 copy.71
  469.5 13.9 %fusion.143 = (f32[4,512]{1,0:T(4,128)S(1)}, f32[4,512,3584]{2,1,0:T(8,128)}) fusion(pred[3584]{0:T(1024)(128)(4,1)S(1)} %broadcast_in_dim.79, bf16[512,4,32]{0,2,1:T(8,128)(2,1)S(1)} %bitcast.268, bf16[3584,4,32]{0,2,1:T(8,128)(2,1)S(1)} %reshape.506), kind=kOutput, calls=%fused_computation.164.clone.1 | convolution fusion | flops 499125760 | bytes 30420480 | tf_op jit(solution)/shard_map/while/body/eval_jaxpr/sub | solution.py:97
  483.4 11.8 %fusion.144 = bf16[4,32,512]{2,1,0:T(8,128)(2,1)S(1)} fusion(bf16[3584,4,32]{0,2,1:T(8,128)(2,1)S(1)} %reshape.505, f32[4,512,3584]{2,1,0:T(8,128)} %get-tuple-element.207, f32[4,512]{1,0:T(4,128)S(1)} %get-tuple-element.208), kind=kOutput, calls=%fused_computation.10.clone.1 | convolution fusion | flops 484507648 | bytes 30416896 | tf_op jit(solution)/shard_map/while/body/eval_jaxpr/hqk,khd->qhd/dot_general | solution.py:99
  496.0 2.4 convolution_add_fusion
  (222 shorter events, 118.1 us)
Async XLA Ops:
  0.0 91.2 %copy-start = (bf16[128,384]{1,0:T(8,128)(2,1)S(1)}, bf16[128,384]{1,0:T(8,128)(2,1)}, u32[]{:S(2)}) copy-start(bf16[128,384]{1,0:T(8,128)(2,1)} %param.25) | copy-start | bytes 294916
  0.0 18.3 %copy-start.3 = (bf16[8,512,128]{2,1,0:T(8,128)(2,1)S(1)}, bf16[8,512,128]{2,1,0:T(8,128)(2,1)}, u32[]{:S(2)}) copy-start(bf16[8,512,128]{2,1,0:T(8,128)(2,1)} %param.21) | copy-start | bytes 3145732
  1.8 20.7 %collective-permute-start = (bf16[8,8,8,128]{3,2,1,0:T(8,128)(2,1)}, bf16[8,8,8,128]{3,2,1,0:T(8,128)(2,1)}, u32[]{:S(2)}, u32[]{:S(2)}) collective-permute-start(bf16[8,8,8,128]{3,2,1,0:T(8,128)(2,1)} %get-tuple-element.167), channel_id=1, source_target_pairs={{0,16},{16,32},{32,48},{48,64},{64,80},{80,96},{96,112},{1,17},{17... | collective-permute-start | bytes 393224 | tf_op jit(solution)/shard_map/ppermute | solution.py:15
  5.6 18.1 %collective-permute-start.1 = (bf16[8,8,8,128]{3,2,1,0:T(8,128)(2,1)}, bf16[8,8,8,128]{3,2,1,0:T(8,128)(2,1)}, u32[]{:S(2)}, u32[]{:S(2)}) collective-permute-start(bf16[8,8,8,128]{3,2,1,0:T(8,128)(2,1)} %get-tuple-element.166), channel_id=1, source_target_pairs={{16,0},{32,16},{48,32},{64,48},{80,64},{96,80},{112,96},{17,1},{33... | collective-permute-start | bytes 393224 | tf_op jit(solution)/shard_map/ppermute | solution.py:15
  9.2 16.3 %collective-permute-start.2 = (bf16[8,8,8,128]{3,2,1,0:T(8,128)(2,1)}, bf16[8,8,8,128]{3,2,1,0:T(8,128)(2,1)}, u32[]{:S(2)}, u32[]{:S(2)}) collective-permute-start(bf16[8,8,8,128]{3,2,1,0:T(8,128)(2,1)} %get-tuple-element.165), channel_id=1, source_target_pairs={{0,1},{1,2},{2,3},{3,4},{4,5},{5,6},{6,7},{7,8},{8,9},{9,10},{10,1... | collective-permute-start | bytes 393224 | tf_op jit(solution)/shard_map/ppermute | solution.py:15
  12.5 14.9 %collective-permute-start.3 = (bf16[8,8,8,128]{3,2,1,0:T(8,128)(2,1)}, bf16[8,8,8,128]{3,2,1,0:T(8,128)(2,1)}, u32[]{:S(2)}, u32[]{:S(2)}) collective-permute-start(bf16[8,8,8,128]{3,2,1,0:T(8,128)(2,1)} %get-tuple-element.164), channel_id=1, source_target_pairs={{1,0},{2,1},{3,2},{4,3},{5,4},{6,5},{7,6},{8,7},{9,8},{10,9},{11,1... | collective-permute-start | bytes 393224 | tf_op jit(solution)/shard_map/ppermute | solution.py:15
  18.3 0.8 copy-start.32
  57.5 1.8 copy-start.29
  57.5 1.8 copy-start.31
  59.4 1.2 copy-start.28
  60.6 1.2 copy-start.27
  61.8 1.2 copy-start.26
  63.0 1.2 copy-start.25
  64.3 1.2 copy-start.24
  65.5 1.2 copy-start.23
  66.7 1.2 copy-start.22
  67.9 1.2 copy-start.21
  69.2 1.2 copy-start.20
  70.4 1.2 copy-start.19
  71.6 1.2 copy-start.18
  72.8 1.2 copy-start.17
  74.1 1.2 copy-start.16
  75.3 1.2 copy-start.15
  76.5 1.2 copy-start.14
  77.7 1.2 copy-start.13
  79.0 1.2 copy-start.12
  80.2 1.2 copy-start.11
  81.4 1.2 copy-start.10
  82.6 1.2 copy-start.9
  83.9 1.2 copy-start.8
  85.1 1.2 copy-start.7
  86.3 1.2 copy-start.6
  87.5 1.2 copy-start.5
  88.8 1.2 copy-start.4
  88.8 1.5 copy-start.30
  91.1 1.3 copy-start.2
  92.5 13.5 %copy-start.35 = (s32[7]{0:T(128)S(1)}, s32[7]{0:T(128)}, u32[]{:S(2)}) copy-start(s32[7]{0:T(128)} %constant.256) | copy-start | bytes 88
  94.0 49.5 %collective-permute-start.7 = (bf16[1,1,8,512,256]{4,3,2,1,0:T(8,128)(2,1)}, bf16[1,1,8,512,256]{4,3,2,1,0:T(8,128)(2,1)}, u32[]{:S(2)}, u32[]{:S(2)}) collective-permute-start(bf16[1,1,8,512,256]{4,3,2,1,0:T(8,128)(2,1)} %bitcast.72), channel_id=1, source_target_pairs={{1,0},{2,1},{3,2},{4,3},{5,4},{6,5},{7,6},{8,7},{9,8},{10,9},{11,1... | collective-permute-start | bytes 6291464 | tf_op jit(solution)/shard_map/ppermute | solution.py:27
  95.9 49.5 %collective-permute-start.4 = (bf16[1,1,8,512,256]{4,3,2,1,0:T(8,128)(2,1)}, bf16[1,1,8,512,256]{4,3,2,1,0:T(8,128)(2,1)}, u32[]{:S(2)}, u32[]{:S(2)}) collective-permute-start(bf16[1,1,8,512,256]{4,3,2,1,0:T(8,128)(2,1)} %bitcast.72), channel_id=1, source_target_pairs={{0,1},{1,2},{2,3},{3,4},{4,5},{5,6},{6,7},{7,8},{8,9},{9,10},{10,1... | collective-permute-start | bytes 6291464 | tf_op jit(solution)/shard_map/ppermute | solution.py:26
  99.3 46.2 %collective-permute-start.6 = (bf16[1,1,8,512,256]{4,3,2,1,0:T(8,128)(2,1)}, bf16[1,1,8,512,256]{4,3,2,1,0:T(8,128)(2,1)}, u32[]{:S(2)}, u32[]{:S(2)}) collective-permute-start(bf16[1,1,8,512,256]{4,3,2,1,0:T(8,128)(2,1)} %bitcast.72), channel_id=1, source_target_pairs={{16,0},{32,16},{48,32},{64,48},{80,64},{96,80},{112,96},{17,1},{33... | collective-permute-start | bytes 6291464 | tf_op jit(solution)/shard_map/ppermute | solution.py:27
  101.2 44.3 %collective-permute-start.5 = (bf16[1,1,8,512,256]{4,3,2,1,0:T(8,128)(2,1)}, bf16[1,1,8,512,256]{4,3,2,1,0:T(8,128)(2,1)}, u32[]{:S(2)}, u32[]{:S(2)}) collective-permute-start(bf16[1,1,8,512,256]{4,3,2,1,0:T(8,128)(2,1)} %bitcast.72), channel_id=1, source_target_pairs={{0,16},{16,32},{32,48},{48,64},{64,80},{80,96},{96,112},{1,17},{17... | collective-permute-start | bytes 6291464 | tf_op jit(solution)/shard_map/ppermute | solution.py:26
  189.8 306.2 %copy-start.33 = (bf16[128,128]{1,0:T(8,128)(2,1)S(1)}, bf16[128,128]{1,0:T(8,128)(2,1)}, u32[]{:S(2)}) copy-start(bf16[128,128]{1,0:T(8,128)(2,1)} %param.26) | copy-start | bytes 98308
  496.0 2.4 copy-start.34
  496.0 3.6 copy-start.1
where the time goes:
time: 510 us; the launch traced here: 500 us
  matrix products  239 us (47%)
  local copies, waits for them, and re-layouts  191 us (37%)
  waiting for transfers between devices  37 us (7%)
  starting transfers between devices  22.9 us (4%)
  other arithmetic  8.14 us (2%)
    sub x8, matrix products, attend_block(): weights = jnp.exp(scores - row_max)  112 us
    dot_general x8, matrix products, attend_block(): jnp.einsum('hqk,khd->qhd', probabilities, v_heads, preferred_element_type...  94 us
    dynamic_slice x32, local copies, waits for them, and re-layouts, body(): attended = lax.map(one_block, (queries, key_sets, key_ok))  57.5 us
    unnamed x74, local copies, waits for them, and re-layouts  47.1 us
    ppermute x2, waiting for transfers between devices, with_halo(): lax.ppermute(initial, axis, [(b, a) for a, b in up])  35 us
    reshape x8, local copies, waits for them, and re-layouts, attend_block(): v_heads = value_rows.reshape(-1, HEADS, head_width)  17.9 us
    dot_general x27, matrix products, convolve(): jnp.dot(window, conv_weight[tap_index], preferred_element_type=jnp.float32)  12.9 us
    slice x2, local copies, waits for them, and re-layouts, convolve(): padded[:, step_x:step_x + SIDE, step_y:step_y + SIDE, step_z:step_z + SIDE]  11.9 us
  transfers between devices with their start and end apart: 8, of which 2 were waited for; matrix products, arithmetic and copies ran while one was open for 3% of the time, Pallas kernels for 0%

commit v1 on v0

v1 whole, which is shorter than its diff:
```python
import functools
import math

import jax
import jax.numpy as jnp
from jax import lax
from jax.experimental import pallas as pl
from jax.experimental.pallas import tpu as pltpu
from jax.sharding import PartitionSpec as P

HEADS = 4
SIDE = 8
LIMIT = 90.0
F32 = jnp.float32
BF16 = jnp.bfloat16
NT = (((1,), (1,)), ((), ()))


def passed_along(value, axis, steps):
    count = lax.axis_size(axis)
    initial, last = (max(0, -steps), min(count, count - steps))
    return lax.ppermute(value, axis, [(source, source + steps) for source in range(initial, last)])


def shifted_z(x, below, above):
    at = lax.broadcasted_iota(jnp.int32, x.shape, 1)
    down = pltpu.roll(jnp.where(at == SIDE - 1, below, x), 1, 1)
    up = pltpu.roll(jnp.where(at == 0, above, x), SIDE - 1, 1)
    return [down, x, up]


def conv_block(b, nb_ref, vox_ref, faces, w_s, a_s, b_s, mixed_ref, normed_ref):
    rows, ch = SIDE * SIDE, vox_ref.shape[-1]

    def picked(ref, face):
        slot = nb_ref[b, face]
        value = ref[jnp.maximum(slot, 0)].astype(F32).reshape(-1, SIDE, ch)
        return jnp.where(slot >= 0, value, 0.0)

    own = vox_ref[b].astype(F32).reshape(rows, SIDE, ch)
    inner = shifted_z(own, picked(vox_ref, 4), picked(vox_ref, 5))
    xm, xp, ym, yp = [shifted_z(picked(ref, f), 0.0, 0.0) for f, ref in enumerate(faces)]
    blank = jnp.zeros((SIDE, ch), F32)
    for e in range(3):
        for s in range(SIDE + 2):
            if s == 0 or s == SIDE + 1:
                mid = (xm if s == 0 else xp)[e].reshape(rows, ch)
                top = bottom = blank
            else:
                mid = inner[e][(s - 1) * SIDE : s * SIDE].reshape(rows, ch)
                top, bottom = ym[e][s - 1], yp[e][s - 1]
            a_s[e, s] = jnp.concatenate([top, mid, bottom], axis=0).astype(BF16)
            b_s[e, s] = mid.astype(BF16)
    acc = None
    for c in range(3):
        for e in range(3):
            pieces = []
            for r in range(4):
                slabs = [
                    b_s[e, 2 * k + r] if c == 1 else a_s[e, 2 * k + r, c * SIDE : c * SIDE + rows]
                    for k in range(4)
                ]
                pieces.append(jnp.concatenate(slabs, axis=0))
            lhs = jnp.concatenate(pieces, axis=1)
            at = (c * 3 + e) * 4 * ch
            part = jnp.dot(lhs, w_s[at : at + 4 * ch], preferred_element_type=F32)
            acc = part if acc is None else acc + part
    for k in range(4):
        for o in range(2):
            x = 2 * k + o
            here = own[x * SIDE : (x + 1) * SIDE].reshape(rows, ch)
            mixed = (here + acc[k * rows : (k + 1) * rows, o * ch : (o + 1) * ch]).astype(BF16)
            mixed_ref[b, x * rows : (x + 1) * rows] = mixed
            wide = mixed.astype(F32)
            square = jnp.mean(wide * wide, axis=-1, keepdims=True)
            normed_ref[b, x * rows : (x + 1) * rows] = (wide * lax.rsqrt(square + 1e-06)).astype(BF16)


def pair_weights(cw_ref, w_s):
    ch = cw_ref.shape[-1]
    for ce in range(9):
        for r in range(4):
            for o in range(2):
                row = (ce * 4 + r) * ch
                tap = r - o
                value = cw_ref[tap * 9 + ce] if 0 <= tap <= 2 else jnp.zeros((ch, ch), BF16)
                w_s[row : row + ch, o * ch : (o + 1) * ch] = value


def conv_kernel(nb_ref, vox_ref, f0, f1, f2, f3, cw_ref, mixed_ref, normed_ref, w_s, a_s, b_s):
    pair_weights(cw_ref, w_s)

    @pl.loop(0, vox_ref.shape[0])
    def _(b):
        conv_block(b, nb_ref, vox_ref, (f0, f1, f2, f3), w_s, a_s, b_s, mixed_ref, normed_ref)


def head_lanes(shape, h, width):
    lane = lax.broadcasted_iota(jnp.int32, shape, len(shape) - 1)
    return (lane // width) == h


def largest_norm(x, width):
    ch = x.shape[-1]
    wide = x.astype(F32)
    i = lax.broadcasted_iota(jnp.int32, (ch, ch), 0) // width
    j = lax.broadcasted_iota(jnp.int32, (ch, ch), 1) // width
    same = jnp.where(i == j, 1.0, 0.0).astype(BF16)
    sums = jnp.dot((wide * wide).astype(BF16), same, preferred_element_type=F32)
    return jnp.max(sums) * 1.02


def put_head_masks(v_ref, slots, width):
    ch = HEADS * width
    for s in range(slots):
        for h in range(HEADS):
            mask = head_lanes((v_ref.shape[2], ch), h, width)
            v_ref[s, h, :, ch:] = jnp.where(mask, 1.0, 0.0).astype(BF16)


def put_key_set(normed, w_ref, k_ref, v_ref, slot, width):
    ch = HEADS * width
    kv = jnp.dot(normed, w_ref[:, ch:], preferred_element_type=F32).astype(BF16)
    keys, values = kv[:, :ch], kv[:, ch:]
    k_ref[slot] = keys
    for h in range(HEADS):
        mask = head_lanes(values.shape, h, width)
        v_ref[slot, h, :, :ch] = jnp.where(mask, values, jnp.zeros_like(values))
    return largest_norm(keys, width)


def put_queries(queries, q_s, width):
    for h in range(HEADS):
        mask = head_lanes(queries.shape, h, width)
        q_s[h] = jnp.where(mask, queries, jnp.zeros_like(queries))


def add_pair(q_s, k_ref, v_ref, slot, acc_s):
    keys = k_ref[slot]
    total = None
    for h in range(HEADS):
        scores = lax.dot_general(q_s[h], keys, NT, preferred_element_type=F32)
        weights = jnp.exp2(scores).astype(BF16)
        part = jnp.dot(weights, v_ref[slot, h], preferred_element_type=F32)
        total = part if total is None else total + part
    acc_s[...] += total


def add_pair_running(q_s, k_ref, v_ref, slot, acc_s, m_s, width):
    keys = k_ref[slot]
    ch = HEADS * width
    for h in range(HEADS):
        scores = lax.dot_general(q_s[h], keys, NT, preferred_element_type=F32)
        old = m_s[:, h * width : h * width + 1]
        new = jnp.maximum(old, jnp.max(scores, axis=1, keepdims=True))
        weights = jnp.exp2(scores - new).astype(BF16)
        part = jnp.dot(weights, v_ref[slot, h], preferred_element_type=F32)
        mask = head_lanes((scores.shape[0], ch), h, width)
        scale = jnp.where(mask, jnp.exp2(old - new), 1.0)
        acc_s[:, :ch] = acc_s[:, :ch] * scale + part[:, :ch]
        acc_s[:, ch:] = acc_s[:, ch:] * scale + part[:, ch:]
        m_s[...] = jnp.where(mask, new, m_s[...])


def local_kernel(
    nb_ref, cnt_ref, normed_ref, w_ref, acc_ref, m_ref, q_ref, fast_ref, qn_ref, k_s, v_s, q_s, kn_s, list_s
):
    b = pl.program_id(0)
    slots, _, ch = normed_ref.shape
    width = ch // HEADS

    @pl.when(b == 0)
    def _():
        put_head_masks(v_s, slots, width)

        @pl.loop(0, cnt_ref[0])
        def _(s):
            kn_s[s] = put_key_set(normed_ref[s], w_ref, k_s, v_s, s, width)

    fast_ref[b] = 1
    qn_ref[b] = 0.0

    @pl.when(b < cnt_ref[0])
    def _():
        factor = math.log2(math.e) / math.sqrt(width)
        queries = jnp.dot(normed_ref[b], w_ref[:, :ch], preferred_element_type=F32)
        queries = (queries * factor).astype(BF16)
        q_ref[0] = queries
        put_queries(queries, q_s, width)
        acc_ref[0] = jnp.zeros(acc_ref.shape[1:], F32)
        list_s[0] = b
        n = jnp.int32(1)
        kn = kn_s[b]
        for face in (4, 5):
            slot = nb_ref[b, face]
            list_s[n] = jnp.maximum(slot, 0)
            n = jnp.where(slot >= 0, n + 1, n)
            kn = jnp.where(slot >= 0, jnp.maximum(kn, kn_s[jnp.maximum(slot, 0)]), kn)
        qn = largest_norm(queries, width)
        fast = qn * kn <= LIMIT * LIMIT
        qn_ref[b] = qn
        fast_ref[b] = fast.astype(jnp.int32)

        @pl.when(fast)
        def _():
            @pl.loop(0, n)
            def _(i):
                add_pair(q_s, k_s, v_s, list_s[i], acc_ref.at[0])

        @pl.when(jnp.logical_not(fast))
        def _():
            m_ref[0] = jnp.full(m_ref.shape[1:], -1e30, F32)

            @pl.loop(0, n)
            def _(i):
                add_pair_running(q_s, k_s, v_s, list_s[i], acc_ref.at[0], m_ref.at[0], width)


def remote_kernel(
    nb_ref, cnt_ref, fast_ref, qn_ref, acc_ref, m_ref, q_ref, mixed_ref, r0, r1, r2, r3, w_ref, wo_ref,
    out_ref, k_s, v_s, q_s, acc_s, m_s
):
    b = pl.program_id(0)
    ch = q_ref.shape[-1]
    width = ch // HEADS

    @pl.when(b == 0)
    def _():
        put_head_masks(v_s, 4, width)

    @pl.when(b >= cnt_ref[0])
    def _():
        out_ref[0] = jnp.zeros(out_ref.shape[1:], out_ref.dtype)

    @pl.when(b < cnt_ref[0])
    def _():
        put_queries(q_ref[0], q_s, width)
        acc_s[...] = acc_ref[0]
        n = jnp.int32(0)
        kn = jnp.float32(0.0)
        for face, ref in enumerate((r0, r1, r2, r3)):
            there = nb_ref[b, face] >= 0

            def put(ref=ref, n=n, kn=kn):
                return jnp.maximum(kn, put_key_set(ref[0], w_ref, k_s, v_s, n, width))

            kn = lax.cond(there, put, lambda kn=kn: kn)
            n = jnp.where(there, n + 1, n)
        local = fast_ref[b] == 1
        fast = jnp.logical_and(local, qn_ref[b] * kn <= LIMIT * LIMIT)

        @pl.when(fast)
        def _():
            @pl.loop(0, n)
            def _(i):
                add_pair(q_s, k_s, v_s, i, acc_s)

        @pl.when(jnp.logical_not(fast))
        def _():
            m_s[...] = jnp.where(local, jnp.zeros(m_s.shape, F32), m_ref[0])

            @pl.loop(0, n)
            def _(i):
                add_pair_running(q_s, k_s, v_s, i, acc_s, m_s, width)

        attended = (acc_s[:, :ch] / acc_s[:, ch:]).astype(BF16)
        moved = jnp.dot(attended, wo_ref[...], preferred_element_type=F32)
        out_ref[0] = (mixed_ref[0].astype(F32) + moved).astype(out_ref.dtype)


def body(voxels, neighbours, block_count, conv_weight, qkv_weight, out_weight):
    blocks, vox, ch = voxels.shape
    cubes = voxels.reshape(blocks, SIDE, SIDE, SIDE, ch)
    faces = [
        passed_along(cubes[:, -1], "gx", 1),
        passed_along(cubes[:, 0], "gx", -1),
        passed_along(cubes[:, :, -1], "gy", 1),
        passed_along(cubes[:, :, 0], "gy", -1),
    ]
    vmem = pl.BlockSpec(memory_space=pltpu.VMEM)
    smem = pl.BlockSpec(memory_space=pltpu.SMEM)
    like = jax.ShapeDtypeStruct(voxels.shape, BF16)
    mixed, normed = pl.pallas_call(
        conv_kernel,
        out_shape=[like, like],
        in_specs=[smem] + [vmem] * 6,
        out_specs=[vmem, vmem],
        scratch_shapes=[
            pltpu.VMEM((36 * ch, 2 * ch), BF16),
            pltpu.VMEM((3, SIDE + 2, SIDE * SIDE + 2 * SIDE, ch), BF16),
            pltpu.VMEM((3, SIDE + 2, SIDE * SIDE, ch), BF16),
        ],
        cost_estimate=pl.CostEstimate(flops=2 * 9 * 256 * 512 * 256 * blocks, bytes_accessed=4 << 20, transcendentals=0),
        name="conv",
    )(neighbours, voxels, *faces, conv_weight)
    received = [
        passed_along(normed, "gx", 1),
        passed_along(normed, "gx", -1),
        passed_along(normed, "gy", 1),
        passed_along(normed, "gy", -1),
    ]

    def block(*tail):
        return pl.BlockSpec((1,) + tail, lambda b, *_: (b, 0, 0))

    def whole(*shape):
        return pl.BlockSpec(shape, lambda b, *_: (0,) * len(shape))

    acc, m, q, fast, qn = pl.pallas_call(
        local_kernel,
        out_shape=[
            jax.ShapeDtypeStruct((blocks, vox, 2 * ch), F32),
            jax.ShapeDtypeStruct((blocks, vox, ch), F32),
            like,
            jax.ShapeDtypeStruct((blocks,), jnp.int32),
            jax.ShapeDtypeStruct((blocks,), F32),
        ],
        grid_spec=pltpu.PrefetchScalarGridSpec(
            num_scalar_prefetch=2,
            grid=(blocks,),
            in_specs=[whole(blocks, vox, ch), whole(ch, 3 * ch)],
            out_specs=[block(vox, 2 * ch), block(vox, ch), block(vox, ch), smem, smem],
            scratch_shapes=[
                pltpu.VMEM((blocks, vox, ch), BF16),
                pltpu.VMEM((blocks, HEADS, vox, 2 * ch), BF16),
                pltpu.VMEM((HEADS, vox, ch), BF16),
                pltpu.SMEM((blocks,), F32),
                pltpu.SMEM((4,), jnp.int32),
            ],
        ),
        cost_estimate=pl.CostEstimate(flops=22 * 2 * 512 * 512 * 128 * 12, bytes_accessed=8 << 20, transcendentals=22 << 20),
        name="local",
    )(neighbours, block_count, normed, qkv_weight)

    def from_neighbour(face):
        return pl.BlockSpec((1, vox, ch), lambda b, nb, *_: (jnp.maximum(nb[b, face], 0), 0, 0))

    return pl.pallas_call(
        remote_kernel,
        out_shape=like,
        grid_spec=pltpu.PrefetchScalarGridSpec(
            num_scalar_prefetch=2,
            grid=(blocks,),
            in_specs=[smem, smem, block(vox, 2 * ch), block(vox, ch), block(vox, ch), block(vox, ch)]
            + [from_neighbour(f) for f in range(4)]
            + [whole(ch, 3 * ch), whole(ch, ch)],
            out_specs=block(vox, ch),
            scratch_shapes=[
                pltpu.VMEM((4, vox, ch), BF16),
                pltpu.VMEM((4, HEADS, vox, 2 * ch), BF16),
                pltpu.VMEM((HEADS, vox, ch), BF16),
                pltpu.VMEM((vox, 2 * ch), F32),
                pltpu.VMEM((vox, ch), F32),
            ],
        ),
        cost_estimate=pl.CostEstimate(flops=9 * 2 * 512 * 512 * 128 * 12, bytes_accessed=8 << 20, transcendentals=9 << 20),
        name="remote",
    )(neighbours, block_count, fast, qn, acc, m, q, mixed, *received, qkv_weight, out_weight)


def solution(mesh):
    placed = (P(("gx", "gy"), None, None), P(("gx", "gy"), None), P(("gx", "gy")), P(), P(), P())
    return jax.shard_map(
        body, mesh=mesh, in_specs=placed, out_specs=P(("gx", "gy"), None, None), check_vma=False
    )
```

time: 510 us -> 154 us (0.30); the launches traced: 500 us -> 156 us
  matrix products: 239 us -> 0 us
  local copies, waits for them, and re-layouts: 191 us -> 4.24 us
  Pallas kernels: 0 us -> 124 us
  waiting for transfers between devices: 37 us -> 1.25 us
  other arithmetic: 8.14 us -> 0 us
    dot_general x44 -> x0, matrix products: 128 us -> none  [the longest x8 94 us: attend_block(): jnp.einsum('hqk,khd->qhd', probabilities, v_heads, preferred_element_type...]
    pallas_call x0 -> x3, Pallas kernels: none -> 124 us  [the longest x1 71.4 us: body(): pl.pallas_call(local_kernel, out_shape=[jax.ShapeDtypeStruct((blocks, vox...]
    sub x8 -> x0, matrix products: 112 us -> none  [attend_block(): weights = jnp.exp(scores - row_max)]
    dynamic_slice x32 -> x0, local copies, waits for them, and re-layouts: 57.5 us -> none  [body(): attended = lax.map(one_block, (queries, key_sets, key_ok))]
    unnamed x74 -> x14, local copies, waits for them, and re-layouts: 47.1 us -> 2.26 us
    ppermute x4 -> x0, waiting for transfers between devices: 37 us -> none  [the longest x2 35 us: with_halo(): lax.ppermute(initial, axis, [(b, a) for a, b in up])]
    slice x14 -> x0, local copies, waits for them, and re-layouts: 27.4 us -> none  [the longest x2 11.9 us: convolve(): padded[:, step_x:step_x + SIDE, step_y:step_y + SIDE, step_z:step_z + SIDE]]
    reshape x16 -> x0, local copies, waits for them, and re-layouts: 26.7 us -> none  [the longest x8 17.9 us: attend_block(): v_heads = value_rows.reshape(-1, HEADS, head_width)]
  transfers between devices with their start and end apart: 8 -> 8, of which waited for: 2 -> 1; matrix products, arithmetic and copies ran while one was open for 3% -> 1% of each run, Pallas kernels for 0% -> 46%
where the time goes in v1:
time: 154 us; the launch traced here: 156 us
  Pallas kernels  124 us (81%)
  starting transfers between devices  25.4 us (16%)
  local copies, waits for them, and re-layouts  4.24 us (3%)
    pallas_call x1, Pallas kernels, body(): pl.pallas_call(local_kernel, out_shape=[jax.ShapeDtypeStruct((blocks, vox...  71.4 us
    pallas_call x1, Pallas kernels, body(): pl.pallas_call(remote_kernel, out_shape=like, grid_spec=pltpu.PrefetchSca...  41.9 us
    ppermute x8, starting transfers between devices, passed_along(): lax.ppermute(value, axis, [(source, source + steps) for source in range(i...  25.4 us
    pallas_call x1, Pallas kernels, body(): pl.pallas_call(conv_kernel, out_shape=[like, like], in_specs=[smem] + [vm...  10.6 us
  transfers between devices with their start and end apart: 8, of which 1 were waited for; matrix products, arithmetic and copies ran while one was open for 1% of the time, Pallas kernels for 46%

profile of v1, /device:TPU:67, one launch (start us, length us, event | category | flops | bytes accessed | tf_op | source)
XLA Modules:
  0.0 155.5 jit_solution(6982540763047895553)
XLA Ops:
  0.0 1.0 slice_bitcast_fusion
  1.0 1.9 %collective-permute-start.3 = (bf16[8,8,8,128]{3,2,1,0:T(8,128)(2,1)S(1)}, bf16[8,8,8,128]{3,2,1,0:T(8,128)(2,1)S(1)}, u32[]{:S(2)}, u32[]{:S(2)}) collective-permute-start(bf16[8,8,8,128]{3,2,1,0:T(8,128)(2,1)S(1)} %get-tuple-element.19), channel_id=1, source_target_pairs={{1,0},{2,1},{3,2},{4,3},{5,4},{6,5},{7,6},{8,7},{9,8},{10,9},{11,1... | collective-permute-start | bytes 393224 | tf_op jit(solution)/shard_map/ppermute | solution.py:22
  2.9 3.4 %collective-permute-start.2 = (bf16[8,8,8,128]{3,2,1,0:T(8,128)(2,1)S(1)}, bf16[8,8,8,128]{3,2,1,0:T(8,128)(2,1)S(1)}, u32[]{:S(2)}, u32[]{:S(2)}) collective-permute-start(bf16[8,8,8,128]{3,2,1,0:T(8,128)(2,1)S(1)} %get-tuple-element.20), channel_id=1, source_target_pairs={{0,1},{1,2},{2,3},{3,4},{4,5},{5,6},{6,7},{7,8},{8,9},{9,10},{10,1... | collective-permute-start | bytes 393224 | tf_op jit(solution)/shard_map/ppermute | solution.py:22
  6.3 1.0 slice_bitcast_fusion.2
  7.3 3.1 %collective-permute-start.1 = (bf16[8,8,8,128]{3,2,1,0:T(8,128)(2,1)S(1)}, bf16[8,8,8,128]{3,2,1,0:T(8,128)(2,1)S(1)}, u32[]{:S(2)}, u32[]{:S(2)}) collective-permute-start(bf16[8,8,8,128]{3,2,1,0:T(8,128)(2,1)S(1)} %get-tuple-element.21), channel_id=1, source_target_pairs={{16,0},{32,16},{48,32},{64,48},{80,64},{96,80},{112,96},{17,1},{33... | collective-permute-start | bytes 393224 | tf_op jit(solution)/shard_map/ppermute | solution.py:22
  10.4 3.1 %collective-permute-start = (bf16[8,8,8,128]{3,2,1,0:T(8,128)(2,1)S(1)}, bf16[8,8,8,128]{3,2,1,0:T(8,128)(2,1)S(1)}, u32[]{:S(2)}, u32[]{:S(2)}) collective-permute-start(bf16[8,8,8,128]{3,2,1,0:T(8,128)(2,1)S(1)} %get-tuple-element.22), channel_id=1, source_target_pairs={{0,16},{16,32},{32,48},{48,64},{64,80},{80,96},{96,112},{1,17},{17... | collective-permute-start | bytes 393224 | tf_op jit(solution)/shard_map/ppermute | solution.py:22
  14.2 0.0 collective-permute-done.3.f3
  14.2 0.0 copy-start.3
  14.2 0.0 collective-permute-done.2.f2
  14.2 0.0 copy-start.4
  14.2 0.0 collective-permute-done.1.f1
  14.3 0.0 copy-start.5
  14.3 1.2 collective-permute-done.f0
  15.5 0.0 copy-done.3
  15.5 0.0 copy-done.4
  15.5 0.0 copy-done.5
  15.5 0.0 copy-start.6
  15.5 0.7 copy-done.6
  16.2 10.6 %conv.1 = (bf16[8,512,128]{2,1,0:T(8,128)(2,1)}, bf16[8,512,128]{2,1,0:T(8,128)(2,1)}) custom-call(s32[8,6]{1,0:T(8,128)} %nb_ref.5, bf16[8,512,128]{2,1,0:T(8,128)(2,1)} %vox_ref.1, bf16[8,8,8,128]{3,2,1,0:T(8,128)(2,1)} %copy-done.6, bf16[8,8,8,128]{3,2,1,0:T(8,128)(2,1)} %copy-done.5, bf16[8,8,8,128]{3,2,1,0:T(8,128)(2,1)} %copy-done.4, ...), custom_call_target="tpu_custom_call" | custom-call | flops 4831838208 | bytes 4194304 | tf_op jit(solution)/shard_map/conv/pallas_call | solution.py:283
  26.8 1.9 %collective-permute-start.7 = (bf16[8,512,128]{2,1,0:T(8,128)(2,1)}, bf16[8,512,128]{2,1,0:T(8,128)(2,1)S(1)}, u32[]{:S(2)}, u32[]{:S(2)}) collective-permute-start(bf16[8,512,128]{2,1,0:T(8,128)(2,1)} %get-tuple-element.12.normed_ref), channel_id=1, source_target_pairs={{1,0},{2,1},{3,2},{4,3},{5,4},{6,5},{7,6},{8,7},{9,8},{10,9},{11,1... | collective-permute-start | bytes 3145736 | tf_op jit(solution)/shard_map/ppermute | solution.py:22
  28.7 5.4 %collective-permute-start.6 = (bf16[8,512,128]{2,1,0:T(8,128)(2,1)}, bf16[8,512,128]{2,1,0:T(8,128)(2,1)S(1)}, u32[]{:S(2)}, u32[]{:S(2)}) collective-permute-start(bf16[8,512,128]{2,1,0:T(8,128)(2,1)} %get-tuple-element.12.normed_ref), channel_id=1, source_target_pairs={{0,1},{1,2},{2,3},{3,4},{4,5},{5,6},{6,7},{7,8},{8,9},{9,10},{10,1... | collective-permute-start | bytes 3145736 | tf_op jit(solution)/shard_map/ppermute | solution.py:22
  34.1 1.9 %collective-permute-start.5 = (bf16[8,512,128]{2,1,0:T(8,128)(2,1)}, bf16[8,512,128]{2,1,0:T(8,128)(2,1)S(1)}, u32[]{:S(2)}, u32[]{:S(2)}) collective-permute-start(bf16[8,512,128]{2,1,0:T(8,128)(2,1)} %get-tuple-element.12.normed_ref), channel_id=1, source_target_pairs={{16,0},{32,16},{48,32},{64,48},{80,64},{96,80},{112,96},{17,1},{33... | collective-permute-start | bytes 3145736 | tf_op jit(solution)/shard_map/ppermute | solution.py:22
  36.0 4.6 %collective-permute-start.4 = (bf16[8,512,128]{2,1,0:T(8,128)(2,1)}, bf16[8,512,128]{2,1,0:T(8,128)(2,1)}, u32[]{:S(2)}, u32[]{:S(2)}) collective-permute-start(bf16[8,512,128]{2,1,0:T(8,128)(2,1)} %get-tuple-element.12.normed_ref), channel_id=1, source_target_pairs={{0,16},{16,32},{32,48},{48,64},{64,80},{80,96},{96,112},{1,17},{17... | collective-permute-start | bytes 3145736 | tf_op jit(solution)/shard_map/ppermute | solution.py:22
  40.6 71.4 %local.1 = (f32[8,512,256]{2,1,0:T(8,128)}, f32[8,512,128]{2,1,0:T(8,128)}, bf16[8,512,128]{2,1,0:T(8,128)(2,1)}, s32[8]{0:T(128)}, f32[8]{0:T(128)}) custom-call(s32[8,6]{1,0:T(8,128)} %nb_ref.5, s32[1]{0:T(128)S(6)} %copy.17.cnt_ref, bf16[8,512,128]{2,1,0:T(8,128)(2,1)} %get-tuple-element.12.normed_ref, bf16[128,384]{1,0:T(8,128)(2,1)} %w_ref.3), custom_call_target="tpu_custom_call" | custom-call | flops 17716740096 | bytes 8388608 | tf_op jit(solution)/shard_map/local/pallas_call | solution.py:309
  112.0 0.0 collective-permute-done.7.r3
  112.0 0.0 copy-start
  112.0 0.0 collective-permute-done.6.r2
  112.0 0.0 copy-start.1
  112.0 0.0 collective-permute-done.5.r1
  112.1 0.0 copy-start.2
  112.1 0.0 collective-permute-done.4.r0
  112.1 0.9 copy-done
  113.0 0.3 copy-done.1
  113.3 0.3 copy-done.2
  113.7 41.9 %remote.1 = bf16[8,512,128]{2,1,0:T(8,128)(2,1)} custom-call(s32[8,6]{1,0:T(8,128)} %nb_ref.5, s32[1]{0:T(128)S(6)} %copy.17.cnt_ref, s32[8]{0:T(128)} %get-tuple-element.13.fast_ref, f32[8]{0:T(128)} %get-tuple-element.14.qn_ref, f32[8,512,256]{2,1,0:T(8,128)} %get-tuple-element.15.acc_ref, f32[8,512,128]{2,1,0:T(8,128)} %get-tuple-element.16.m_ref, ...), custom_call_target="tpu_custom_call" | custom-call | flops 7247757312 | bytes 8388608 | tf_op jit(solution)/shard_map/remote/pallas_call | solution.py:338
Async XLA Ops:
  1.0 13.2 %collective-permute-start.3 = (bf16[8,8,8,128]{3,2,1,0:T(8,128)(2,1)S(1)}, bf16[8,8,8,128]{3,2,1,0:T(8,128)(2,1)S(1)}, u32[]{:S(2)}, u32[]{:S(2)}) collective-permute-start(bf16[8,8,8,128]{3,2,1,0:T(8,128)(2,1)S(1)} %get-tuple-element.19), channel_id=1, source_target_pairs={{1,0},{2,1},{3,2},{4,3},{5,4},{6,5},{7,6},{8,7},{9,8},{10,9},{11,1... | collective-permute-start | bytes 393224 | tf_op jit(solution)/shard_map/ppermute | solution.py:22
  2.9 11.3 %collective-permute-start.2 = (bf16[8,8,8,128]{3,2,1,0:T(8,128)(2,1)S(1)}, bf16[8,8,8,128]{3,2,1,0:T(8,128)(2,1)S(1)}, u32[]{:S(2)}, u32[]{:S(2)}) collective-permute-start(bf16[8,8,8,128]{3,2,1,0:T(8,128)(2,1)S(1)} %get-tuple-element.20), channel_id=1, source_target_pairs={{0,1},{1,2},{2,3},{3,4},{4,5},{5,6},{6,7},{7,8},{8,9},{9,10},{10,1... | collective-permute-start | bytes 393224 | tf_op jit(solution)/shard_map/ppermute | solution.py:22
  7.3 7.0 %collective-permute-start.1 = (bf16[8,8,8,128]{3,2,1,0:T(8,128)(2,1)S(1)}, bf16[8,8,8,128]{3,2,1,0:T(8,128)(2,1)S(1)}, u32[]{:S(2)}, u32[]{:S(2)}) collective-permute-start(bf16[8,8,8,128]{3,2,1,0:T(8,128)(2,1)S(1)} %get-tuple-element.21), channel_id=1, source_target_pairs={{16,0},{32,16},{48,32},{64,48},{80,64},{96,80},{112,96},{17,1},{33... | collective-permute-start | bytes 393224 | tf_op jit(solution)/shard_map/ppermute | solution.py:22
  10.4 5.0 %collective-permute-start = (bf16[8,8,8,128]{3,2,1,0:T(8,128)(2,1)S(1)}, bf16[8,8,8,128]{3,2,1,0:T(8,128)(2,1)S(1)}, u32[]{:S(2)}, u32[]{:S(2)}) collective-permute-start(bf16[8,8,8,128]{3,2,1,0:T(8,128)(2,1)S(1)} %get-tuple-element.22), channel_id=1, source_target_pairs={{0,16},{16,32},{32,48},{48,64},{64,80},{80,96},{96,112},{1,17},{17... | collective-permute-start | bytes 393224 | tf_op jit(solution)/shard_map/ppermute | solution.py:22
  14.2 1.3 copy-start.3
  14.2 1.3 copy-start.4
  14.3 1.2 copy-start.5
  15.5 0.7 copy-start.6
  26.8 85.2 %collective-permute-start.7 = (bf16[8,512,128]{2,1,0:T(8,128)(2,1)}, bf16[8,512,128]{2,1,0:T(8,128)(2,1)S(1)}, u32[]{:S(2)}, u32[]{:S(2)}) collective-permute-start(bf16[8,512,128]{2,1,0:T(8,128)(2,1)} %get-tuple-element.12.normed_ref), channel_id=1, source_target_pairs={{1,0},{2,1},{3,2},{4,3},{5,4},{6,5},{7,6},{8,7},{9,8},{10,9},{11,1... | collective-permute-start | bytes 3145736 | tf_op jit(solution)/shard_map/ppermute | solution.py:22
  28.7 83.3 %collective-permute-start.6 = (bf16[8,512,128]{2,1,0:T(8,128)(2,1)}, bf16[8,512,128]{2,1,0:T(8,128)(2,1)S(1)}, u32[]{:S(2)}, u32[]{:S(2)}) collective-permute-start(bf16[8,512,128]{2,1,0:T(8,128)(2,1)} %get-tuple-element.12.normed_ref), channel_id=1, source_target_pairs={{0,1},{1,2},{2,3},{3,4},{4,5},{5,6},{6,7},{7,8},{8,9},{9,10},{10,1... | collective-permute-start | bytes 3145736 | tf_op jit(solution)/shard_map/ppermute | solution.py:22
  34.1 78.0 %collective-permute-start.5 = (bf16[8,512,128]{2,1,0:T(8,128)(2,1)}, bf16[8,512,128]{2,1,0:T(8,128)(2,1)S(1)}, u32[]{:S(2)}, u32[]{:S(2)}) collective-permute-start(bf16[8,512,128]{2,1,0:T(8,128)(2,1)} %get-tuple-element.12.normed_ref), channel_id=1, source_target_pairs={{16,0},{32,16},{48,32},{64,48},{80,64},{96,80},{112,96},{17,1},{33... | collective-permute-start | bytes 3145736 | tf_op jit(solution)/shard_map/ppermute | solution.py:22
  36.0 76.1 %collective-permute-start.4 = (bf16[8,512,128]{2,1,0:T(8,128)(2,1)}, bf16[8,512,128]{2,1,0:T(8,128)(2,1)}, u32[]{:S(2)}, u32[]{:S(2)}) collective-permute-start(bf16[8,512,128]{2,1,0:T(8,128)(2,1)} %get-tuple-element.12.normed_ref), channel_id=1, source_target_pairs={{0,16},{16,32},{32,48},{48,64},{64,80},{80,96},{96,112},{1,17},{17... | collective-permute-start | bytes 3145736 | tf_op jit(solution)/shard_map/ppermute | solution.py:22
  112.0 1.0 copy-start
  112.0 1.3 copy-start.1
  112.1 1.6 %copy-start.2 = (bf16[8,512,128]{2,1,0:T(8,128)(2,1)}, bf16[8,512,128]{2,1,0:T(8,128)(2,1)S(1)}, u32[]{:S(2)}) copy-start(bf16[8,512,128]{2,1,0:T(8,128)(2,1)S(1)} %collective-permute-done.5.r1) | copy-start | bytes 3145732
